TPU v7x, 32 devices: a whole 2x2x4 slice. The times are simulated.
32 devices in a mesh: dp: 4 (over y, core), seq: 8 (over z, x).
Axes of the slice: x: 2, y: 2, z: 4, core: 2. Of those that a mesh axis runs over, the one named last changes fastest.
Arguments:
- layer_input: bfloat16 [4096, 8192], P(('dp', 'seq')), may hold values from -6 to 6
- queries: bfloat16 [4096, 4096], P(('dp', 'seq')), may hold values from -110 to 110, as said below
- key_states: bfloat16 [4096, 512], P(('dp', 'seq')), may hold values from -12 to 12, as said below
- value_states: bfloat16 [4096, 512], P(('dp', 'seq')), may hold values from -6 to 6
- out_grad: bfloat16 [4096, 4096], P(('dp', 'seq')), may hold values from -6 to 6
Outputs:
- query_grad: bfloat16 [4096, 4096], P(('dp', 'seq'))
- key_grad: bfloat16 [4096, 512], P(('dp', 'seq'))
- value_grad: bfloat16 [4096, 512], P(('dp', 'seq'))
- weight_grad: float32 [8192, 1024], P(('dp', 'seq'))
Inputs may be any that keep to these rules, and one draw needn't show every extreme that they name: `queries`: rows of rough scales; some queries may nearly coincide in direction with keys of earlier positions. `key_states`: rows of rough scales.
All inputs are finite; a program needn't handle non-finite values.
Results may differ from a plain program's by a relative error of at most 0.0051.
Values may be sent and summed in bfloat16 or wider, within the bound.
No kernel may reach another device: no remote copies, remote signals or barrier semaphores. Data moves between devices by JAX's collectives and lax.ppermute only.
A program may use at most 128 MiB of HBM per device.

v0:
```python
import math
import jax
import jax.numpy as jnp
from jax import lax
from jax.sharding import PartitionSpec as P

D = 8192
QH = 32
KVH = 4
HD = 128
NEGATIVE = -1e30


def local(layer_input, queries, key_states, value_states, out_grad):
    local_rows = layer_input.shape[0]
    cycle_size = lax.axis_size("seq")
    replicas = lax.axis_size("dp")
    position = lax.axis_index("seq")
    length = local_rows * cycle_size
    group = QH // KVH
    channels = KVH * HD
    scale = 1.0 / math.sqrt(HD)
    block = math.gcd(length, 512)
    key_all, value_all = (
        lax.all_gather(key_states, "seq", axis=0, tiled=True),
        lax.all_gather(value_states, "seq", axis=0, tiled=True),
    )
    query_heads = queries.reshape(local_rows, KVH, group, HD)
    grad_heads = out_grad.reshape(local_rows, KVH, group, HD)
    query_place = position * local_rows + jnp.arange(local_rows, dtype=jnp.int32)
    needed = (position * local_rows + local_rows + block - 1) // block

    def block_scores(begin):
        key_block = lax.dynamic_slice_in_dim(key_all, begin, block, 0).reshape(block, KVH, HD)
        value_block = lax.dynamic_slice_in_dim(value_all, begin, block, 0).reshape(block, KVH, HD)
        scores = (
            jnp.einsum("tkgd,skd->kgts", query_heads, key_block, preferred_element_type=jnp.float32)
            * scale
        )
        key_place = begin + jnp.arange(block, dtype=jnp.int32)
        visible = key_place[None, :] <= query_place[:, None]
        scores = jnp.where(visible, scores, NEGATIVE)
        grad_probs = jnp.einsum(
            "tkgd,skd->kgts", grad_heads, value_block, preferred_element_type=jnp.float32
        )
        return (key_block, scores, grad_probs)

    def first_pass(step_index, carry):
        row_max, denom, weighted = carry
        key_block, scores, grad_probs = block_scores(step_index * block)
        new_max = jnp.maximum(row_max, jnp.max(scores, axis=-1))
        factor = jnp.exp(row_max - new_max)
        expon = jnp.exp(scores - new_max[..., None])
        return (
            new_max,
            denom * factor + jnp.sum(expon, axis=-1),
            weighted * factor + jnp.sum(expon * grad_probs, axis=-1),
        )

    stats_shape = (KVH, group, local_rows)
    start_stats = (
        jnp.full(stats_shape, NEGATIVE, jnp.float32),
        jnp.zeros(stats_shape, jnp.float32),
        jnp.zeros(stats_shape, jnp.float32),
    )
    row_max, denom, weighted = lax.fori_loop(0, needed, first_pass, start_stats)
    delta = weighted / denom

    def second_pass(step_index, carry):
        grad_query, terms = carry
        begin = step_index * block
        key_block, scores, grad_probs = block_scores(begin)
        probs = jnp.exp(scores - row_max[..., None]) / denom[..., None]
        grad_scores = (scale * probs * (grad_probs - delta[..., None])).astype(jnp.bfloat16)
        probs_low = probs.astype(jnp.bfloat16)
        grad_query = grad_query + jnp.einsum(
            "kgts,skd->tkgd", grad_scores, key_block, preferred_element_type=jnp.float32
        )
        key_part = jnp.einsum(
            "kgts,tkgd->skd", grad_scores, query_heads, preferred_element_type=jnp.float32
        )
        value_part = jnp.einsum(
            "kgts,tkgd->skd", probs_low, grad_heads, preferred_element_type=jnp.float32
        )
        joined = jnp.concatenate(
            [key_part.reshape(block, channels), value_part.reshape(block, channels)], axis=1
        )
        terms = lax.dynamic_update_slice_in_dim(terms, joined, begin, 0)
        return (grad_query, terms)

    start_grads = (
        jnp.zeros((local_rows, KVH, group, HD), jnp.float32),
        jnp.zeros((length, 2 * channels), jnp.float32),
    )
    grad_query, terms = lax.fori_loop(0, needed, second_pass, start_grads)
    query_grad = grad_query.reshape(local_rows, QH * HD).astype(jnp.bfloat16)
    owned_grads = lax.psum_scatter(terms, "seq", scatter_dimension=0, tiled=True).astype(
        jnp.bfloat16
    )
    summed_grads = lax.all_gather(owned_grads, "seq", axis=0, tiled=True)
    slab = D // (replicas * cycle_size)
    columns = lax.all_to_all(
        layer_input.reshape(local_rows, replicas, cycle_size, slab),
        "seq",
        split_axis=2,
        concat_axis=0,
        tiled=True,
    )
    columns = columns.reshape(length, replicas * slab)
    weight_grad = lax.psum_scatter(
        jnp.einsum("tr,tc->rc", columns, summed_grads, preferred_element_type=jnp.float32),
        "dp",
        scatter_dimension=0,
        tiled=True,
    )
    return (query_grad, owned_grads[:, :channels], owned_grads[:, channels:], weight_grad)


def solution(mesh):
    in_specs = (
        P(("dp", "seq"), None),
        P(("dp", "seq"), None),
        P(("dp", "seq"), None),
        P(("dp", "seq"), None),
        P(("dp", "seq"), None),
    )
    out_specs = (
        P(("dp", "seq"), None),
        P(("dp", "seq"), None),
        P(("dp", "seq"), None),
        P(("dp", "seq"), None),
    )
    return jax.shard_map(local, mesh=mesh, in_specs=in_specs, out_specs=out_specs, check_vma=False)
```

profile of v0, /device:TPU:0, one launch (start us, length us, event | category | flops | bytes accessed | tf_op | source)
XLA Modules:
  0.0 388.9 jit_solution(6068416372018879133)
XLA Ops:
  7.2 1.7 copy.69
  8.9 1.7 copy.71
  10.7 1.6 copy.70
  13.0 1.6 copy.72
  15.9 37.0 %all-gather.4.cloned.1.call-done = bf16[1024,512]{0,1:T(8,128)(2,1)} async-done(((bf16[128,512]{0,1:T(8,128)(2,1)}), bf16[1024,512]{0,1:T(8,128)(2,1)}) %all-gather.4.cloned.1.call-update) | async-done | bytes 1048592 | tf_op jit(solution)/shard_map/all_gather | solution.py:25
  52.9 41.1 %all-gather.6.cloned.1.call-done = bf16[1024,512]{0,1:T(8,128)(2,1)} async-done(((bf16[128,512]{0,1:T(8,128)(2,1)}), bf16[1024,512]{0,1:T(8,128)(2,1)}) %all-gather.6.cloned.1.call-update) | async-done | bytes 1048592 | tf_op jit(solution)/shard_map/all_gather | solution.py:26
  94.0 7.5 %while.28 = (s32[]{:T(128)}, f32[4,8,128]{2,1,0:T(8,128)S(1)}, f32[4,8,128]{2,1,0:T(8,128)S(1)}, f32[4,8,128]{2,1,0:T(8,128)S(1)}, s32[]{:T(128)}, /*index=5*/bf...) while((s32[]{:T(128)}, f32[4,8,128]{2,1,0:T(8,128)S(1)}, ...), condition=%wide.region_4.5_spmd.clone, body=%wide.region_0.4_spmd.clone.sunk | while | flops 1098986112 | bytes 35165400 | solution.py:66
  96.9 1.8 fusion.59
  98.7 2.7 fusion.58
  101.5 2.5 broadcast_in_dim.32.clone
  104.0 1.6 broadcast_in_dim.31
  105.6 19.8 %while.29 = (s32[]{:T(128)}, f32[128,4,8,128]{0,3,2,1:T(8,128)}, f32[1024,1024]{1,0:T(8,128)}, s32[]{:T(128)}, bf16[1024,512]{0,1:T(8,128)(2,1)}, /*index=5*/bf1...) while((s32[]{:T(128)}, f32[128,4,8,128]{0,3,2,1:T(8,128)}, ...), condition=%wide.region_6.7_spmd.clone, body=%wide.region_5.6_spmd.clone.sunk | while | flops 2704343552 | bytes 108713312 | solution.py:95
  105.6 1.6 constant_dynamic-slice_fusion.7
  107.4 2.3 fusion.70
  109.8 1.7 fusion.71
  111.5 1.5 fusion.73
  113.4 1.5 fusion.72
  114.9 1.5 pad_maximum_fusion.2
  116.4 1.9 copy.110
  118.4 1.5 constant_dynamic-update-slice_fusion.2
  121.3 4.1 %bitcast_add_fusion.2 = f32[128,4,8,128]{0,3,2,1:T(8,128)} fusion(f32[128,4,8,128]{0,3,2,1:T(8,128)} %get-tuple-element.501, bf16[512,4,128,1]{0,2,3,1:T(8,128)(2,1)} %bitcast.153, bf16[4,8,128,512]{2,3,1,0:T(8,128)(2,1)S(1)} %copy-done.1), kind=kOutput, calls=%fused_computation.26.clone.1 | convolution fusion | flops 537395200 | bytes 8912896 | tf_op jit(solution)/shard_map/while/body/kgts,skd->tkgd/dot_general | solution.py:76
  125.4 3.2 copy.77
  128.6 1.5 copy.78
  130.1 30.8 %all-to-all-start = ((bf16[128,4,8,256]{0,3,1,2:T(8,128)(2,1)}), bf16[128,4,8,256]{0,3,1,2:T(8,128)(2,1)S(1)}, u32[]{:S(2)}, u32[]{:S(2)}) async-start(bf16[128,4,8,256]{0,3,1,2:T(8,128)(2,1)} %copy.78), calls=%async_computation.1 | async-start | bytes 4194304 | tf_op jit(solution)/shard_map/all_to_all | solution.py:102
  161.0 117.2 %reduce-scatter.3.cloned.1.call-done = f32[128,1024]{1,0:T(8,128)} async-done(((f32[1024,1024]{1,0:T(8,128)}), f32[128,1024]{1,0:T(8,128)}) %reduce-scatter.3.cloned.1.call-update) | async-done | bytes 524304 | tf_op jit(solution)/shard_map/reduce_scatter | solution.py:97
  278.2 1.8 convert_element_type.17
  280.3 2.7 copy.79
  283.0 47.1 %all-gather.8.cloned.1.call-done = bf16[1024,1024]{1,0:T(8,128)(2,1)} async-done(((bf16[128,1024]{1,0:T(8,128)(2,1)}), bf16[1024,1024]{1,0:T(8,128)(2,1)}) %all-gather.8.cloned.1.call-update) | async-done | bytes 2097168 | tf_op jit(solution)/shard_map/all_gather | solution.py:100
  330.0 6.6 %convolution_bitcast_fusion = f32[1024,1024]{0,1:T(8,128)} fusion(bf16[1024,1024]{1,0:T(8,128)(2,1)} %all-gather.8.cloned.1.call-done, bf16[128,8,8,128]{3,2,1,0:T(8,128)(2,1)} %bitcast.159), kind=kOutput, calls=%fused_computation.33 | convolution fusion | flops 2147483648 | bytes 8388608 | tf_op jit(solution)/shard_map/tr,tc->rc/dot_general | solution.py:111
  336.6 1.6 copy-done.2
  340.4 39.4 %reduce-scatter.5.cloned.1.call-done = f32[256,1024]{0,1:T(8,128)} async-done(((f32[1024,1024]{0,1:T(8,128)}), f32[256,1024]{0,1:T(8,128)}) %reduce-scatter.5.cloned.1.call-update) | async-done | bytes 1048592 | tf_op jit(solution)/shard_map/reduce_scatter | solution.py:110
  379.8 2.5 copy.80
  (46 shorter events, 9.7 us)
Async XLA Ops:
  7.2 45.7 %all-gather.4.cloned.1.call-start = ((), (), s32[]{:S(2)}) async-start(), calls=%async_computation.3 | async-start | bytes 1179648 | tf_op jit(solution)/shard_map/all_gather | solution.py:25
  8.9 85.1 %all-gather.6.cloned.1.call-start = ((), (), s32[]{:S(2)}) async-start(), calls=%async_computation.4 | async-start | bytes 1179648 | tf_op jit(solution)/shard_map/all_gather | solution.py:26
  10.6 267.5 %reduce-scatter.3.cloned.1.call-start = ((), (), s32[]{:S(2)}) async-start(), calls=%async_computation.5 | async-start | bytes 4718592 | tf_op jit(solution)/shard_map/reduce_scatter | solution.py:97
  96.9 1.8 copy-start.7
  105.6 5.8 %copy-start.3 = (bf16[128,4,8,128]{0,3,2,1:T(8,128)(2,1)}, bf16[128,4,8,128]{0,3,2,1:T(8,128)(2,1)S(1)}, u32[]{:S(2)}) copy-start(bf16[128,4,8,128]{0,3,2,1:T(8,128)(2,1)S(1)} %get-tuple-element.521) | copy-start | bytes 3145732 | tf_op jit(solution)/shard_map/while
  107.2 2.5 copy-start.5
  111.5 2.0 copy-start
  118.3 2.9 copy-start.1
  121.3 4.1 %copy-start.4 = (bf16[128,4,8,128]{0,3,2,1:T(8,128)(2,1)S(1)}, bf16[128,4,8,128]{0,3,2,1:T(8,128)(2,1)}, u32[]{:S(2)}) copy-start(bf16[128,4,8,128]{0,3,2,1:T(8,128)(2,1)} %copy-done.3) | copy-start | bytes 3145732 | tf_op jit(solution)/shard_map/while
  130.1 150.1 %all-to-all-start = ((bf16[128,4,8,256]{0,3,1,2:T(8,128)(2,1)}), bf16[128,4,8,256]{0,3,1,2:T(8,128)(2,1)S(1)}, u32[]{:S(2)}, u32[]{:S(2)}) async-start(bf16[128,4,8,256]{0,3,1,2:T(8,128)(2,1)} %copy.78), calls=%async_computation.1 | async-start | bytes 4194304 | tf_op jit(solution)/shard_map/all_to_all | solution.py:102
  160.9 169.1 %all-gather.8.cloned.1.call-start = ((), (), s32[]{:S(2)}) async-start(), calls=%async_computation.6 | async-start | bytes 2359296 | tf_op jit(solution)/shard_map/all_gather | solution.py:100
  280.0 99.8 %reduce-scatter.5.cloned.1.call-start = ((), (), s32[]{:S(2)}) async-start(), calls=%async_computation.7 | async-start | bytes 5242880 | tf_op jit(solution)/shard_map/reduce_scatter | solution.py:110
  336.6 1.6 copy-start.2
  336.6 3.1 copy-start.6
Sparse Core Ops, SparseCore 0:
  10.6 42.2 all-gather.3
  55.5 38.4 all-gather.5
  125.5 152.5 reduce-scatter.2
  280.9 49.0 all-gather.7
  336.8 42.9 reduce-scatter.4
where the time goes:
time: 390 us; the launch traced here: 389 us
  waiting for transfers between devices  282 us (72%)
  local copies, waits for them, and re-layouts  34.5 us (9%)
  starting transfers between devices  31.2 us (8%)
  matrix products  21.8 us (6%)
  between operations  13.9 us (4%)
  other arithmetic  5.56 us (1%)
    reduce_scatter x1, waiting for transfers between devices, local(): lax.psum_scatter(terms, 'seq', scatter_dimension=0, tiled=True)  117 us
    all_gather x1, waiting for transfers between devices, local(): summed_grads = lax.all_gather(owned_grads, 'seq', axis=0, tiled=True)  47.1 us
    all_gather x1, waiting for transfers between devices, local(): lax.all_gather(value_states, 'seq', axis=0, tiled=True)  41.1 us
    reduce_scatter x1, waiting for transfers between devices, local(): lax.psum_scatter(jnp.einsum('tr,tc->rc', columns, summed_grads, preferred...  39.4 us
    all_gather x1, waiting for transfers between devices, local(): lax.all_gather(key_states, 'seq', axis=0, tiled=True)  37 us
    all_to_all x1, starting transfers between devices, local(): lax.all_to_all(layer_input.reshape(local_rows, replicas, cycle_size, slab...  30.8 us
    unnamed x12, local copies, waits for them, and re-layouts  15.9 us
  transfers between devices with their start and end apart: 6, of which 5 were waited for; matrix products, arithmetic and copies ran while one was open for 5% of the time, Pallas kernels for 0%

commit v1 on v0

--- a/solution.py
+++ b/solution.py
@@ -97,7 +97,12 @@
     owned_grads = lax.psum_scatter(terms, "seq", scatter_dimension=0, tiled=True).astype(
         jnp.bfloat16
     )
-    summed_grads = lax.all_gather(owned_grads, "seq", axis=0, tiled=True)
+    ring = [owned_grads]
+    for hop in range(7):
+        ring.append(lax.ppermute(ring[-1], "seq", [(dev, (dev + 1) % 8) for dev in range(8)]))
+    summed_grads = jnp.roll(
+        jnp.concatenate(ring[::-1], axis=0), (lax.axis_index("seq") + 1) * ring[0].shape[0], axis=0
+    )
     slab = D // (replicas * cycle_size)
     columns = lax.all_to_all(
         layer_input.reshape(local_rows, replicas, cycle_size, slab),

time: 390 us -> 410 us (1.051)
  waiting for transfers between devices: 282 us -> 298 us
  local copies, waits for them, and re-layouts: 34.5 us -> 39.4 us
    ppermute x0 -> x7, waiting for transfers between devices: none -> 64.4 us  [local(): lax.ppermute(ring[-1], 'seq', [(dev, (dev + 1) % 8) for dev in range(8)])]
    all_gather x1 -> x0, waiting for transfers between devices: 47.1 us -> none  [local(): summed_grads = lax.all_gather(owned_grads, 'seq', axis=0, tiled=True)]
    unnamed x12 -> x38, local copies, waits for them, and re-layouts: 15.9 us -> 22.1 us
  transfers between devices with their start and end apart: 6 -> 12, of which waited for: 5 -> 11; matrix products, arithmetic and copies ran while one was open for 5% -> 4% of each run, Pallas kernels for 0% -> 0%
where the time goes in v1:
time: 410 us; the launch traced here: 409 us
  waiting for transfers between devices  298 us (73%)
  local copies, waits for them, and re-layouts  39.4 us (10%)
  starting transfers between devices  32.6 us (8%)
  matrix products  19.6 us (5%)
  between operations  14 us (3%)
  other arithmetic  4.99 us (1%)
    reduce_scatter x1, waiting for transfers between devices, local(): lax.psum_scatter(terms, 'seq', scatter_dimension=0, tiled=True)  117 us
    ppermute x7, waiting for transfers between devices, local(): lax.ppermute(ring[-1], 'seq', [(dev, (dev + 1) % 8) for dev in range(8)])  64.4 us
    all_gather x1, waiting for transfers between devices, local(): lax.all_gather(value_states, 'seq', axis=0, tiled=True)  41.1 us
    reduce_scatter x1, waiting for transfers between devices, local(): lax.psum_scatter(jnp.einsum('tr,tc->rc', columns, summed_grads, preferred...  38.1 us
    all_gather x1, waiting for transfers between devices, local(): lax.all_gather(key_states, 'seq', axis=0, tiled=True)  37 us
    all_to_all x1, starting transfers between devices, local(): lax.all_to_all(layer_input.reshape(local_rows, replicas, cycle_size, slab...  30.9 us
    unnamed x38, local copies, waits for them, and re-layouts  22.1 us
  transfers between devices with their start and end apart: 12, of which 11 were waited for; matrix products, arithmetic and copies ran while one was open for 4% of the time, Pallas kernels for 0%

profile of v1, /device:TPU:0, one launch (start us, length us, event | category | flops | bytes accessed | tf_op | source)
XLA Modules:
  0.0 408.8 jit_solution(1612613472445662216)
XLA Ops:
  7.2 1.7 copy.69
  8.9 1.7 copy.71
  10.7 1.6 copy.70
  13.0 1.6 copy.72
  15.9 37.0 %all-gather.3.cloned.1.call-done = bf16[1024,512]{0,1:T(8,128)(2,1)} async-done(((bf16[128,512]{0,1:T(8,128)(2,1)}), bf16[1024,512]{0,1:T(8,128)(2,1)}) %all-gather.3.cloned.1.call-update) | async-done | bytes 1048592 | tf_op jit(solution)/shard_map/all_gather | solution.py:25
  52.9 41.1 %all-gather.5.cloned.1.call-done = bf16[1024,512]{0,1:T(8,128)(2,1)} async-done(((bf16[128,512]{0,1:T(8,128)(2,1)}), bf16[1024,512]{0,1:T(8,128)(2,1)}) %all-gather.5.cloned.1.call-update) | async-done | bytes 1048592 | tf_op jit(solution)/shard_map/all_gather | solution.py:26
  94.0 7.5 %while.28 = (s32[]{:T(128)}, f32[4,8,128]{2,1,0:T(8,128)S(1)}, f32[4,8,128]{2,1,0:T(8,128)S(1)}, f32[4,8,128]{2,1,0:T(8,128)S(1)}, s32[]{:T(128)}, /*index=5*/bf...) while((s32[]{:T(128)}, f32[4,8,128]{2,1,0:T(8,128)S(1)}, ...), condition=%wide.region_4.5_spmd.clone, body=%wide.region_0.4_spmd.clone.sunk | while | flops 1098986112 | bytes 35165400 | solution.py:66
  96.9 1.8 fusion.60
  98.7 2.7 fusion.59
  101.5 2.5 broadcast_in_dim.32.clone
  104.0 1.6 broadcast_in_dim.31
  105.6 19.9 %while.29 = (s32[]{:T(128)}, f32[128,4,8,128]{0,3,2,1:T(8,128)}, f32[1024,1024]{1,0:T(8,128)}, s32[]{:T(128)}, bf16[1024,512]{0,1:T(8,128)(2,1)}, /*index=5*/bf1...) while((s32[]{:T(128)}, f32[128,4,8,128]{0,3,2,1:T(8,128)}, ...), condition=%wide.region_6.7_spmd.clone, body=%wide.region_5.6_spmd.clone.sunk | while | flops 2704343552 | bytes 108713312 | solution.py:95
  105.6 1.6 constant_dynamic-slice_fusion.7
  107.4 2.3 fusion.71
  109.8 1.7 fusion.72
  116.5 1.9 copy.110
  121.3 4.1 %bitcast_add_fusion.2 = f32[128,4,8,128]{0,3,2,1:T(8,128)} fusion(f32[128,4,8,128]{0,3,2,1:T(8,128)} %get-tuple-element.501, bf16[512,4,128,1]{0,2,3,1:T(8,128)(2,1)} %bitcast.152, bf16[4,8,128,512]{2,3,1,0:T(8,128)(2,1)S(1)} %copy-done.1), kind=kOutput, calls=%fused_computation.26.clone.1 | convolution fusion | flops 537395200 | bytes 8912896 | tf_op jit(solution)/shard_map/while/body/kgts,skd->tkgd/dot_general | solution.py:76
  125.5 3.2 copy.77
  130.2 30.9 %all-to-all-start = ((bf16[128,4,8,256]{0,3,1,2:T(8,128)(2,1)}), bf16[128,4,8,256]{0,3,1,2:T(8,128)(2,1)S(1)}, u32[]{:S(2)}, u32[]{:S(2)}) async-start(bf16[128,4,8,256]{0,3,1,2:T(8,128)(2,1)} %copy.78), calls=%async_computation.1 | async-start | bytes 4194304 | tf_op jit(solution)/shard_map/all_to_all | solution.py:107
  161.1 117.5 %reduce-scatter.3.cloned.1.call-done = f32[128,1024]{1,0:T(8,128)} async-done(((f32[1024,1024]{1,0:T(8,128)}), f32[128,1024]{1,0:T(8,128)}) %reduce-scatter.3.cloned.1.call-update) | async-done | bytes 524304 | tf_op jit(solution)/shard_map/reduce_scatter | solution.py:97
  279.7 1.5 collective-permute-start
  281.3 9.3 %collective-permute-done = bf16[128,1024]{1,0:T(8,128)(2,1)S(1)} collective-permute-done((bf16[128,1024]{1,0:T(8,128)(2,1)S(1)}, bf16[128,1024]{1,0:T(8,128)(2,1)S(1)}, u32[]{:S(2)}, u32[]{:S(2)}) %collective-permute-start) | collective-permute-done | bytes 262176 | tf_op jit(solution)/shard_map/ppermute | solution.py:102
  290.6 9.9 %collective-permute-done.1 = bf16[128,1024]{1,0:T(8,128)(2,1)S(1)} collective-permute-done((bf16[128,1024]{1,0:T(8,128)(2,1)S(1)}, bf16[128,1024]{1,0:T(8,128)(2,1)S(1)}, u32[]{:S(2)}, u32[]{:S(2)}) %collective-permute-start.1) | collective-permute-done | bytes 262176 | tf_op jit(solution)/shard_map/ppermute | solution.py:102
  300.5 9.1 %collective-permute-done.2 = bf16[128,1024]{1,0:T(8,128)(2,1)S(1)} collective-permute-done((bf16[128,1024]{1,0:T(8,128)(2,1)S(1)}, bf16[128,1024]{1,0:T(8,128)(2,1)S(1)}, u32[]{:S(2)}, u32[]{:S(2)}) %collective-permute-start.2) | collective-permute-done | bytes 262176 | tf_op jit(solution)/shard_map/ppermute | solution.py:102
  310.3 9.1 %collective-permute-done.3 = bf16[128,1024]{1,0:T(8,128)(2,1)S(1)} collective-permute-done((bf16[128,1024]{1,0:T(8,128)(2,1)S(1)}, bf16[128,1024]{1,0:T(8,128)(2,1)S(1)}, u32[]{:S(2)}, u32[]{:S(2)}) %collective-permute-start.3) | collective-permute-done | bytes 262176 | tf_op jit(solution)/shard_map/ppermute | solution.py:102
  320.0 9.1 %collective-permute-done.4 = bf16[128,1024]{1,0:T(8,128)(2,1)S(1)} collective-permute-done((bf16[128,1024]{1,0:T(8,128)(2,1)S(1)}, bf16[128,1024]{1,0:T(8,128)(2,1)S(1)}, u32[]{:S(2)}, u32[]{:S(2)}) %collective-permute-start.4) | collective-permute-done | bytes 262176 | tf_op jit(solution)/shard_map/ppermute | solution.py:102
  329.8 10.0 %collective-permute-done.5 = bf16[128,1024]{1,0:T(8,128)(2,1)} collective-permute-done((bf16[128,1024]{1,0:T(8,128)(2,1)S(1)}, bf16[128,1024]{1,0:T(8,128)(2,1)}, u32[]{:S(2)}, u32[]{:S(2)}) %collective-permute-start.5) | collective-permute-done | bytes 262176 | tf_op jit(solution)/shard_map/ppermute | solution.py:102
  341.2 8.0 %collective-permute-done.6 = bf16[128,1024]{1,0:T(8,128)(2,1)} collective-permute-done((bf16[128,1024]{1,0:T(8,128)(2,1)}, bf16[128,1024]{1,0:T(8,128)(2,1)}, u32[]{:S(2)}, u32[]{:S(2)}) %collective-permute-start.6) | collective-permute-done | bytes 262176 | tf_op jit(solution)/shard_map/ppermute | solution.py:102
  353.5 4.3 %convolution_bitcast_fusion = f32[1024,1024]{0,1:T(8,128)} fusion(bf16[128,8,8,128]{3,2,1,0:T(8,128)(2,1)S(1)} %bitcast.158, bf16[2048,1024]{1,0:T(8,128)(2,1)S(1)} %constant_dynamic-update-slice_fusion.1, s32[]{:T(128)S(6)} %select_n.35), kind=kOutput, calls=%fused_computation.33 | convolution fusion | flops 2147483648 | bytes 8388612 | tf_op jit(solution)/shard_map/tr,tc->rc/dot_general | solution.py:116
  357.8 1.6 copy-done.2
  361.6 38.1 %reduce-scatter.5.cloned.1.call-done = f32[256,1024]{0,1:T(8,128)} async-done(((f32[1024,1024]{0,1:T(8,128)}), f32[256,1024]{0,1:T(8,128)}) %reduce-scatter.5.cloned.1.call-update) | async-done | bytes 1048592 | tf_op jit(solution)/shard_map/reduce_scatter | solution.py:115
  399.7 2.5 copy.80
  (85 shorter events, 25.6 us)
Async XLA Ops:
  7.2 45.7 %all-gather.3.cloned.1.call-start = ((), (), s32[]{:S(2)}) async-start(), calls=%async_computation.3 | async-start | bytes 1179648 | tf_op jit(solution)/shard_map/all_gather | solution.py:25
  8.9 85.1 %all-gather.5.cloned.1.call-start = ((), (), s32[]{:S(2)}) async-start(), calls=%async_computation.4 | async-start | bytes 1179648 | tf_op jit(solution)/shard_map/all_gather | solution.py:26
  10.6 267.9 %reduce-scatter.3.cloned.1.call-start = ((), (), s32[]{:S(2)}) async-start(), calls=%async_computation.5 | async-start | bytes 4718592 | tf_op jit(solution)/shard_map/reduce_scatter | solution.py:97
  96.9 1.8 copy-start.7
  105.6 5.8 %copy-start.3 = (bf16[128,4,8,128]{0,3,2,1:T(8,128)(2,1)}, bf16[128,4,8,128]{0,3,2,1:T(8,128)(2,1)S(1)}, u32[]{:S(2)}) copy-start(bf16[128,4,8,128]{0,3,2,1:T(8,128)(2,1)S(1)} %get-tuple-element.521) | copy-start | bytes 3145732 | tf_op jit(solution)/shard_map/while
  107.2 2.5 copy-start.5
  111.5 2.0 copy-start
  118.4 2.9 copy-start.1
  121.3 4.1 %copy-start.4 = (bf16[128,4,8,128]{0,3,2,1:T(8,128)(2,1)S(1)}, bf16[128,4,8,128]{0,3,2,1:T(8,128)(2,1)}, u32[]{:S(2)}) copy-start(bf16[128,4,8,128]{0,3,2,1:T(8,128)(2,1)} %copy-done.3) | copy-start | bytes 3145732 | tf_op jit(solution)/shard_map/while
  130.2 209.6 %all-to-all-start = ((bf16[128,4,8,256]{0,3,1,2:T(8,128)(2,1)}), bf16[128,4,8,256]{0,3,1,2:T(8,128)(2,1)S(1)}, u32[]{:S(2)}, u32[]{:S(2)}) async-start(bf16[128,4,8,256]{0,3,1,2:T(8,128)(2,1)} %copy.78), calls=%async_computation.1 | async-start | bytes 4194304 | tf_op jit(solution)/shard_map/all_to_all | solution.py:107
  161.1 238.7 %reduce-scatter.5.cloned.1.call-start = ((), (), s32[]{:S(2)}) async-start(), calls=%async_computation.6 | async-start | bytes 5242880 | tf_op jit(solution)/shard_map/reduce_scatter | solution.py:115
  278.6 72.7 %copy-start.6 = (f32[128,1024]{1,0:T(8,128)S(1)}, f32[128,1024]{1,0:T(8,128)}, u32[]{:S(2)}) copy-start(f32[128,1024]{1,0:T(8,128)} %reduce-scatter.3.cloned.1.call-done) | copy-start | bytes 1572868
  279.7 10.8 %collective-permute-start = (bf16[128,1024]{1,0:T(8,128)(2,1)S(1)}, bf16[128,1024]{1,0:T(8,128)(2,1)S(1)}, u32[]{:S(2)}, u32[]{:S(2)}) collective-permute-start(bf16[128,1024]{1,0:T(8,128)(2,1)S(1)} %convert_element_type.17), channel_id=1, source_target_pairs={{0,1},{1,2},{2,3},{3,4},{4,5},{5,6},{6,7},{7,0},{8,9},{9,10},{10,1... | collective-permute-start | bytes 786440 | tf_op jit(solution)/shard_map/ppermute | solution.py:102
  290.6 9.9 %collective-permute-start.1 = (bf16[128,1024]{1,0:T(8,128)(2,1)S(1)}, bf16[128,1024]{1,0:T(8,128)(2,1)S(1)}, u32[]{:S(2)}, u32[]{:S(2)}) collective-permute-start(bf16[128,1024]{1,0:T(8,128)(2,1)S(1)} %collective-permute-done), channel_id=1, source_target_pairs={{0,1},{1,2},{2,3},{3,4},{4,5},{5,6},{6,7},{7,0},{8,9},{9,10},{10,1... | collective-permute-start | bytes 786440 | tf_op jit(solution)/shard_map/ppermute | solution.py:102
  300.5 9.1 %collective-permute-start.2 = (bf16[128,1024]{1,0:T(8,128)(2,1)S(1)}, bf16[128,1024]{1,0:T(8,128)(2,1)S(1)}, u32[]{:S(2)}, u32[]{:S(2)}) collective-permute-start(bf16[128,1024]{1,0:T(8,128)(2,1)S(1)} %collective-permute-done.1), channel_id=1, source_target_pairs={{0,1},{1,2},{2,3},{3,4},{4,5},{5,6},{6,7},{7,0},{8,9},{9,10},{10,1... | collective-permute-start | bytes 786440 | tf_op jit(solution)/shard_map/ppermute | solution.py:102
  309.5 0.7 copy-start.8
  310.2 9.1 %collective-permute-start.3 = (bf16[128,1024]{1,0:T(8,128)(2,1)S(1)}, bf16[128,1024]{1,0:T(8,128)(2,1)S(1)}, u32[]{:S(2)}, u32[]{:S(2)}) collective-permute-start(bf16[128,1024]{1,0:T(8,128)(2,1)S(1)} %collective-permute-done.2), channel_id=1, source_target_pairs={{0,1},{1,2},{2,3},{3,4},{4,5},{5,6},{6,7},{7,0},{8,9},{9,10},{10,1... | collective-permute-start | bytes 786440 | tf_op jit(solution)/shard_map/ppermute | solution.py:102
  319.3 0.7 copy-start.10
  320.0 9.1 %collective-permute-start.4 = (bf16[128,1024]{1,0:T(8,128)(2,1)S(1)}, bf16[128,1024]{1,0:T(8,128)(2,1)S(1)}, u32[]{:S(2)}, u32[]{:S(2)}) collective-permute-start(bf16[128,1024]{1,0:T(8,128)(2,1)S(1)} %collective-permute-done.3), channel_id=1, source_target_pairs={{0,1},{1,2},{2,3},{3,4},{4,5},{5,6},{6,7},{7,0},{8,9},{9,10},{10,1... | collective-permute-start | bytes 786440 | tf_op jit(solution)/shard_map/ppermute | solution.py:102
  329.1 0.7 copy-start.12
  329.8 10.0 %collective-permute-start.5 = (bf16[128,1024]{1,0:T(8,128)(2,1)S(1)}, bf16[128,1024]{1,0:T(8,128)(2,1)}, u32[]{:S(2)}, u32[]{:S(2)}) collective-permute-start(bf16[128,1024]{1,0:T(8,128)(2,1)S(1)} %collective-permute-done.4), channel_id=1, source_target_pairs={{0,1},{1,2},{2,3},{3,4},{4,5},{5,6},{6,7},{7,0},{8,9},{9,10},{10,1... | collective-permute-start | bytes 786440 | tf_op jit(solution)/shard_map/ppermute | solution.py:102
  339.8 9.4 %collective-permute-start.6 = (bf16[128,1024]{1,0:T(8,128)(2,1)}, bf16[128,1024]{1,0:T(8,128)(2,1)}, u32[]{:S(2)}, u32[]{:S(2)}) collective-permute-start(bf16[128,1024]{1,0:T(8,128)(2,1)} %collective-permute-done.5), channel_id=1, source_target_pairs={{0,1},{1,2},{2,3},{3,4},{4,5},{5,6},{6,7},{7,0},{8,9},{9,10},{10,1... | collective-permute-start | bytes 786440 | tf_op jit(solution)/shard_map/ppermute | solution.py:102
  339.8 11.3 %copy-start.13 = (bf16[128,1024]{1,0:T(8,128)(2,1)S(1)}, bf16[128,1024]{1,0:T(8,128)(2,1)}, u32[]{:S(2)}) copy-start(bf16[128,1024]{1,0:T(8,128)(2,1)} %copy-done.12) | copy-start | bytes 786436
  339.8 11.4 %copy-start.11 = (bf16[128,1024]{1,0:T(8,128)(2,1)S(1)}, bf16[128,1024]{1,0:T(8,128)(2,1)}, u32[]{:S(2)}) copy-start(bf16[128,1024]{1,0:T(8,128)(2,1)} %copy-done.10) | copy-start | bytes 786436
  339.8 11.4 %copy-start.9 = (bf16[128,1024]{1,0:T(8,128)(2,1)S(1)}, bf16[128,1024]{1,0:T(8,128)(2,1)}, u32[]{:S(2)}) copy-start(bf16[128,1024]{1,0:T(8,128)(2,1)} %copy-done.8) | copy-start | bytes 786436
  357.8 1.6 copy-start.2
Sparse Core Ops, SparseCore 0:
  10.6 42.2 all-gather.2
  55.5 38.4 all-gather.4
  125.6 152.9 reduce-scatter.2
  358.0 41.7 reduce-scatter.4
